TPU v7x, 32 devices: a whole 2x2x4 slice. The times are simulated.
32 devices in a mesh: fx: 8 (over z, x), fy: 4 (over y, core).
Axes of the slice: x: 2, y: 2, z: 4, core: 2. Of those that a mesh axis runs over, the one named last changes fastest.
Arguments:
- right_side: float32 [512, 2048], P(('fx', 'fy'))
- coupling: float32 [512, 11, 4096], P(('fx', 'fy')), may hold values from -0.109375 to 0.109375
- face_columns: int32 [512, 11], P(('fx', 'fy')), may hold values from 0 to 31, as said below
- ghost_lists: int32 [128, 4], P(('fx', 'fy')), may hold values from 0 to 15, as said below
Outputs:
- solution: float32 [512, 2048], P(('fx', 'fy'))
- residual: float32 [512, 2048], P(('fx', 'fy'))
Inputs may be any that keep to these rules, and one draw needn't show every extreme that they name: face_columns[f, 0] is f's own index within its block; entries 1 to 6 name other faces of the same block, all distinct and below 16; entries 7 to 10 are distinct and name received faces, 16 + d * 4 + g for the g-th face of group d of the extended list; every received slot of every block is named by some row of that block. `ghost_lists`: each row names 4 distinct faces of its block by local index.
All inputs are finite; a program needn't handle non-finite values.
Results may differ from a plain program's by a relative error of at most 0.0003.
Values sent between devices are 32-bit elements; how exact they have to be, the bound alone decides.
A program may use at most 64 MiB of HBM per device.

v0:
```python
import jax
import jax.numpy as jnp
from jax import lax
from jax.sharding import PartitionSpec as P

DOF = 64
NRHS = 32
BLOCKS = 11
POWERS = 3


def from_behind(block, axis, distance):
    devices = range(lax.axis_size(axis))
    route = [(i - distance, i) for i in devices if i - distance in devices]
    return lax.ppermute(block, axis, route)


def receive_rows(field, ghost_lists):
    from_lower_x = from_behind(jnp.take(field, ghost_lists[1], axis=0), "fx", 1)
    from_upper_x = from_behind(jnp.take(field, ghost_lists[0], axis=0), "fx", -1)
    from_lower_y = from_behind(jnp.take(field, ghost_lists[3], axis=0), "fy", 1)
    from_upper_y = from_behind(jnp.take(field, ghost_lists[2], axis=0), "fy", -1)
    return jnp.concatenate([from_lower_x, from_upper_x, from_lower_y, from_upper_y], axis=0)


def contract(block_mats, picked):
    face_count = picked.shape[0]
    shaped = picked.reshape(face_count, picked.shape[1], DOF, NRHS)
    result = jnp.einsum("fkab,fkbr->far", block_mats, shaped, precision=lax.Precision.HIGHEST)
    return result.reshape(face_count, DOF * NRHS)


def solve_small(gram_total):
    count = NRHS
    row_ids = jnp.arange((POWERS + 1) * count)[:, None]
    col_ids = jnp.arange(POWERS * count)[None, :]
    shift_map = ((row_ids == col_ids) | (row_ids == col_ids + count)).astype(jnp.float32)
    first = (row_ids == jnp.arange(count)[None, :]).astype(jnp.float32)
    high = lax.Precision.HIGHEST
    normal_matrix = jnp.dot(
        shift_map.T, jnp.dot(gram_total, shift_map, precision=high), precision=high
    )
    right_terms = jnp.dot(shift_map.T, gram_total[:, :count], precision=high)
    factor = jnp.linalg.cholesky(normal_matrix)
    coeffs = jax.scipy.linalg.cho_solve((factor, True), right_terms)
    combo = first - jnp.dot(shift_map, coeffs, precision=high)
    return (coeffs, combo)


def on_device(right_side, coupling, face_columns, ghost_lists):
    face_count = right_side.shape[0]
    block_mats = coupling.reshape(face_count, BLOCKS, DOF, DOF)
    high = lax.Precision.HIGHEST

    def as_rows(field):
        return field.reshape(face_count * DOF, NRHS)

    fields = [right_side]
    partial_grams = []
    for power_index in range(POWERS + 1):
        if power_index > 0:
            power_field = fields[-1]
            received = receive_rows(power_field, ghost_lists)
            extended = jnp.concatenate([power_field, received], axis=0)
            fields.append(contract(block_mats, jnp.take(extended, face_columns, axis=0)))
        earlier_rows = jnp.concatenate([as_rows(item) for item in fields], axis=1)
        local_block = jnp.dot(
            earlier_rows.T, as_rows(fields[-1]), precision=high, preferred_element_type=jnp.float32
        )
        partial_grams.append(lax.psum(local_block, ("fx", "fy")))
    total_cols = (POWERS + 1) * NRHS
    upper_part = jnp.concatenate(
        [
            jnp.concatenate(
                [item, jnp.zeros((total_cols - item.shape[0], NRHS), jnp.float32)], axis=0
            )
            for item in partial_grams
        ],
        axis=1,
    )
    block_index = jnp.arange(total_cols) // NRHS
    gram_total = jnp.where(block_index[:, None] <= block_index[None, :], upper_part, upper_part.T)
    stacked = jnp.concatenate([as_rows(item) for item in fields], axis=1)
    coeffs, combo = solve_small(gram_total)
    solution = jnp.dot(stacked[:, : POWERS * NRHS], coeffs, precision=high)
    residual = jnp.dot(stacked, combo, precision=high)
    return (solution.reshape(face_count, DOF * NRHS), residual.reshape(face_count, DOF * NRHS))


def solution(mesh):
    placed = (
        P(("fx", "fy"), None),
        P(("fx", "fy"), None, None),
        P(("fx", "fy"), None),
        P(("fx", "fy"), None),
    )
    return jax.shard_map(
        on_device,
        mesh=mesh,
        in_specs=placed,
        out_specs=(P(("fx", "fy"), None), P(("fx", "fy"), None)),
        check_vma=False,
    )
```

profile of v0, /device:TPU:0, one launch (start us, length us, event | category | flops | bytes accessed | tf_op | source)
XLA Modules:
  0.0 199.0 jit_solution(18109654426102840548)
XLA Ops:
  1.5 1.5 gather_fusion
  3.1 4.9 %collective-permute-start = (f32[4,2048]{1,0:T(4,128)S(1)}, f32[4,2048]{1,0:T(4,128)S(1)}, u32[]{:S(2)}, u32[]{:S(2)}) collective-permute-start(f32[4,2048]{1,0:T(4,128)S(1)} %broadcast_select_fusion.14), channel_id=1, source_target_pairs={{0,4},{4,8},{8,12},{12,16},{16,20},{20,24},{24,28},{1,5},{5,9},{9,... | collective-permute-start | bytes 98312 | tf_op jit(solution)/shard_map/ppermute | solution.py:15
  20.3 5.7 %reshape.92 = f32[16,11,64,64]{3,2,0,1:T(8,128)} reshape(f32[16,11,4096]{2,0,1:T(8,128)} %param.9) | data formatting | bytes 5767168 | tf_op jit(solution)/shard_map/reshape | solution.py:52
  27.3 1.5 reshape.248
  28.9 1.8 broadcast_select_fusion.2
  30.7 3.6 %reshape.276 = f32[16,11,64,32]{3,2,1,0:T(8,128)} reshape(f32[16,11,2048]{2,1,0:T(8,128)S(1)} %broadcast_select_fusion.2) | data formatting | bytes 2883584 | tf_op jit(solution)/shard_map/reshape | solution.py:28
  34.2 12.0 %fusion.6 = f32[16,64,32]{1,2,0:T(8,128)S(1)} fusion(f32[16,11,64,64]{3,2,0,1:T(8,128)} %reshape.92, f32[16,11,64,32]{3,2,1,0:T(8,128)} %reshape.276), kind=kOutput, calls=%fused_computation.21 | convolution fusion | flops 276824064 | bytes 4456448 | tf_op jit(solution)/shard_map/fkab,fkbr->far/dot_general | solution.py:29
  50.6 4.6 %collective-permute-start.6 = (f32[4,2048]{1,0:T(4,128)S(1)}, f32[4,2048]{1,0:T(4,128)S(1)}, u32[]{:S(2)}, u32[]{:S(2)}) collective-permute-start(f32[4,2048]{1,0:T(4,128)S(1)} %broadcast_select_fusion.8), channel_id=1, source_target_pairs={{0,1},{1,2},{2,3},{4,5},{5,6},{6,7},{8,9},{9,10},{10,11},{12,13},{... | collective-permute-start | bytes 98312 | tf_op jit(solution)/shard_map/ppermute | solution.py:15
  56.7 5.3 %collective-permute-start.4 = (f32[4,2048]{1,0:T(4,128)S(1)}, f32[4,2048]{1,0:T(4,128)S(1)}, u32[]{:S(2)}, u32[]{:S(2)}) collective-permute-start(f32[4,2048]{1,0:T(4,128)S(1)} %broadcast_select_fusion.10), channel_id=1, source_target_pairs={{0,4},{4,8},{8,12},{12,16},{16,20},{20,24},{24,28},{1,5},{5,9},{9,... | collective-permute-start | bytes 98312 | tf_op jit(solution)/shard_map/ppermute | solution.py:15
  64.8 1.5 reshape.260
  66.3 1.8 broadcast_select_fusion.1
  68.1 3.6 %reshape.277 = f32[16,11,64,32]{3,2,1,0:T(8,128)} reshape(f32[16,11,2048]{2,1,0:T(8,128)S(1)} %broadcast_select_fusion.1) | data formatting | bytes 2883584 | tf_op jit(solution)/shard_map/reshape | solution.py:28
  71.7 12.0 %fusion.9 = f32[16,64,32]{1,2,0:T(8,128)S(1)} fusion(f32[16,11,64,64]{3,2,0,1:T(8,128)} %reshape.92, f32[16,11,64,32]{3,2,1,0:T(8,128)} %reshape.277), kind=kOutput, calls=%fused_computation.22 | convolution fusion | flops 276824064 | bytes 4456448 | tf_op jit(solution)/shard_map/fkab,fkbr->far/dot_general | solution.py:29
  86.7 4.0 %collective-permute-start.10 = (f32[4,2048]{1,0:T(4,128)S(1)}, f32[4,2048]{1,0:T(4,128)S(1)}, u32[]{:S(2)}, u32[]{:S(2)}) collective-permute-start(f32[4,2048]{1,0:T(4,128)S(1)} %broadcast_select_fusion.4), channel_id=1, source_target_pairs={{0,1},{1,2},{2,3},{4,5},{5,6},{6,7},{8,9},{9,10},{10,11},{12,13},{... | collective-permute-start | bytes 98312 | tf_op jit(solution)/shard_map/ppermute | solution.py:15
  92.2 4.8 %collective-permute-start.8 = (f32[4,2048]{1,0:T(4,128)S(1)}, f32[4,2048]{1,0:T(4,128)S(1)}, u32[]{:S(2)}, u32[]{:S(2)}) collective-permute-start(f32[4,2048]{1,0:T(4,128)S(1)} %broadcast_select_fusion.6), channel_id=1, source_target_pairs={{0,4},{4,8},{8,12},{12,16},{16,20},{20,24},{24,28},{1,5},{5,9},{9,... | collective-permute-start | bytes 98312 | tf_op jit(solution)/shard_map/ppermute | solution.py:15
  97.1 1.5 collective-permute-start.9
  100.2 2.8 %collective-permute-done.9 = f32[4,2048]{1,0:T(4,128)S(1)} collective-permute-done((f32[4,2048]{1,0:T(4,128)S(1)}, f32[4,2048]{1,0:T(4,128)S(1)}, u32[]{:S(2)}, u32[]{:S(2)}) %collective-permute-start.9) | collective-permute-done | bytes 32800 | tf_op jit(solution)/shard_map/ppermute | solution.py:15
  104.3 1.6 reshape.272
  105.9 3.2 %broadcast_select_fusion = f32[16,11,2048]{2,1,0:T(8,128)} fusion(f32[16,11,2048]{2,1,0:T(8,128)} %reshape.272, pred[16,11]{1,0:T(8,128)(4,1)S(1)} %compare_and_fusion), kind=kLoop, calls=%fused_computation.25 | loop fusion | flops 360448 | bytes 2883760 | tf_op jit(solution)/shard_map/jit(_take)/select_n | solution.py:65
  109.2 5.2 %reshape.278 = f32[16,11,64,32]{3,2,1,0:T(8,128)} reshape(f32[16,11,2048]{2,1,0:T(8,128)} %broadcast_select_fusion) | data formatting | bytes 2883584 | tf_op jit(solution)/shard_map/reshape | solution.py:28
  114.3 12.0 %fusion.12 = f32[16,64,32]{1,2,0:T(8,128)S(1)} fusion(f32[16,11,64,64]{3,2,0,1:T(8,128)} %reshape.92, f32[16,11,64,32]{3,2,1,0:T(8,128)} %reshape.278), kind=kOutput, calls=%fused_computation.23 | convolution fusion | flops 276824064 | bytes 4456448 | tf_op jit(solution)/shard_map/fkab,fkbr->far/dot_general | solution.py:29
  128.3 48.2 %all-reduce.3 = (f32[96,32]{1,0:T(8,128)S(1)}, f32[64,32]{1,0:T(8,128)S(1)}, f32[32,32]{1,0:T(8,128)S(1)}, f32[128,32]{1,0:T(8,128)S(1)}) all-reduce(f32[96,32]{1,0:T(8,128)S(1)} %fusion.39, f32[64,32]{1,0:T(8,128)S(1)} %fusion.15, f32[32,32]{1,0:T(8,128)S(1)} %fusion.40, ...), channel_id=1, replica_groups=mesh['fx'=8,'fy'=4] {'fx','fy'}, use_global_device_ids=true, to_apply=%region_2.5 | all-reduce | flops 10240 | bytes 81920 | tf_op jit(solution)/shard_map/psum | solution.py:70
  177.7 8.8 %cholesky.16 = f32[96,96]{1,0:T(8,128)S(1)} custom-call(f32[96,96]{1,0:T(8,128)S(1)} %fusion.30), custom_call_target="Cholesky" | custom-call | tf_op jit(solution)/shard_map/jit(cholesky)/cholesky | solution.py:44
  187.8 7.4 %custom-call.10 = f32[1,96,96]{1,2,0:T(8,128)S(1)} custom-call(f32[1,96,96]{2,1,0:T(8,128)S(1)} %fusion.25), custom_call_target="InvertDiagBlocksLowerTriangular" | custom-call | tf_op jit(solution)/shard_map/jit(_cho_solve)/triangular_solve | solution.py:45
  (96 shorter events, 38.4 us)
Async XLA Ops:
  3.1 23.0 %collective-permute-start = (f32[4,2048]{1,0:T(4,128)S(1)}, f32[4,2048]{1,0:T(4,128)S(1)}, u32[]{:S(2)}, u32[]{:S(2)}) collective-permute-start(f32[4,2048]{1,0:T(4,128)S(1)} %broadcast_select_fusion.14), channel_id=1, source_target_pairs={{0,4},{4,8},{8,12},{12,16},{16,20},{20,24},{24,28},{1,5},{5,9},{9,... | collective-permute-start | bytes 98312 | tf_op jit(solution)/shard_map/ppermute | solution.py:15
  9.5 16.5 %collective-permute-start.1 = (f32[4,2048]{1,0:T(4,128)S(1)}, f32[4,2048]{1,0:T(4,128)S(1)}, u32[]{:S(2)}, u32[]{:S(2)}) collective-permute-start(f32[4,2048]{1,0:T(4,128)S(1)} %broadcast_select_fusion.13), channel_id=1, source_target_pairs={{4,0},{8,4},{12,8},{16,12},{20,16},{24,20},{28,24},{5,1},{9,5},{13... | collective-permute-start | bytes 98312 | tf_op jit(solution)/shard_map/ppermute | solution.py:15
  12.4 13.7 %collective-permute-start.2 = (f32[4,2048]{1,0:T(4,128)S(1)}, f32[4,2048]{1,0:T(4,128)S(1)}, u32[]{:S(2)}, u32[]{:S(2)}) collective-permute-start(f32[4,2048]{1,0:T(4,128)S(1)} %broadcast_select_fusion.12), channel_id=1, source_target_pairs={{0,1},{1,2},{2,3},{4,5},{5,6},{6,7},{8,9},{9,10},{10,11},{12,13},{... | collective-permute-start | bytes 98312 | tf_op jit(solution)/shard_map/ppermute | solution.py:15
  15.4 10.6 %collective-permute-start.3 = (f32[4,2048]{1,0:T(4,128)S(1)}, f32[4,2048]{1,0:T(4,128)S(1)}, u32[]{:S(2)}, u32[]{:S(2)}) collective-permute-start(f32[4,2048]{1,0:T(4,128)S(1)} %broadcast_select_fusion.11), channel_id=1, source_target_pairs={{1,0},{2,1},{3,2},{5,4},{6,5},{7,6},{9,8},{10,9},{11,10},{13,12},{... | collective-permute-start | bytes 98312 | tf_op jit(solution)/shard_map/ppermute | solution.py:15
  20.3 5.8 %copy-start = (f32[16,2048]{1,0:T(8,128)S(1)}, f32[16,2048]{1,0:T(8,128)}, u32[]{:S(2)}) copy-start(f32[16,2048]{1,0:T(8,128)} %param.8) | copy-start | bytes 393220
  49.3 14.3 %collective-permute-start.5 = (f32[4,2048]{1,0:T(4,128)S(1)}, f32[4,2048]{1,0:T(4,128)S(1)}, u32[]{:S(2)}, u32[]{:S(2)}) collective-permute-start(f32[4,2048]{1,0:T(4,128)S(1)} %broadcast_select_fusion.9), channel_id=1, source_target_pairs={{4,0},{8,4},{12,8},{16,12},{20,16},{24,20},{28,24},{5,1},{9,5},{13... | collective-permute-start | bytes 98312 | tf_op jit(solution)/shard_map/ppermute | solution.py:15
  50.6 12.9 %collective-permute-start.6 = (f32[4,2048]{1,0:T(4,128)S(1)}, f32[4,2048]{1,0:T(4,128)S(1)}, u32[]{:S(2)}, u32[]{:S(2)}) collective-permute-start(f32[4,2048]{1,0:T(4,128)S(1)} %broadcast_select_fusion.8), channel_id=1, source_target_pairs={{0,1},{1,2},{2,3},{4,5},{5,6},{6,7},{8,9},{9,10},{10,11},{12,13},{... | collective-permute-start | bytes 98312 | tf_op jit(solution)/shard_map/ppermute | solution.py:15
  55.3 8.2 %collective-permute-start.7 = (f32[4,2048]{1,0:T(4,128)S(1)}, f32[4,2048]{1,0:T(4,128)S(1)}, u32[]{:S(2)}, u32[]{:S(2)}) collective-permute-start(f32[4,2048]{1,0:T(4,128)S(1)} %broadcast_select_fusion.7), channel_id=1, source_target_pairs={{1,0},{2,1},{3,2},{5,4},{6,5},{7,6},{9,8},{10,9},{11,10},{13,12},{... | collective-permute-start | bytes 98312 | tf_op jit(solution)/shard_map/ppermute | solution.py:15
  56.7 6.9 %collective-permute-start.4 = (f32[4,2048]{1,0:T(4,128)S(1)}, f32[4,2048]{1,0:T(4,128)S(1)}, u32[]{:S(2)}, u32[]{:S(2)}) collective-permute-start(f32[4,2048]{1,0:T(4,128)S(1)} %broadcast_select_fusion.10), channel_id=1, source_target_pairs={{0,4},{4,8},{8,12},{12,16},{16,20},{20,24},{24,28},{1,5},{5,9},{9,... | collective-permute-start | bytes 98312 | tf_op jit(solution)/shard_map/ppermute | solution.py:15
  86.7 13.5 %collective-permute-start.10 = (f32[4,2048]{1,0:T(4,128)S(1)}, f32[4,2048]{1,0:T(4,128)S(1)}, u32[]{:S(2)}, u32[]{:S(2)}) collective-permute-start(f32[4,2048]{1,0:T(4,128)S(1)} %broadcast_select_fusion.4), channel_id=1, source_target_pairs={{0,1},{1,2},{2,3},{4,5},{5,6},{6,7},{8,9},{9,10},{10,11},{12,13},{... | collective-permute-start | bytes 98312 | tf_op jit(solution)/shard_map/ppermute | solution.py:15
  90.8 9.4 %collective-permute-start.11 = (f32[4,2048]{1,0:T(4,128)S(1)}, f32[4,2048]{1,0:T(4,128)S(1)}, u32[]{:S(2)}, u32[]{:S(2)}) collective-permute-start(f32[4,2048]{1,0:T(4,128)S(1)} %broadcast_select_fusion.3), channel_id=1, source_target_pairs={{1,0},{2,1},{3,2},{5,4},{6,5},{7,6},{9,8},{10,9},{11,10},{13,12},{... | collective-permute-start | bytes 98312 | tf_op jit(solution)/shard_map/ppermute | solution.py:15
  92.2 8.1 %collective-permute-start.8 = (f32[4,2048]{1,0:T(4,128)S(1)}, f32[4,2048]{1,0:T(4,128)S(1)}, u32[]{:S(2)}, u32[]{:S(2)}) collective-permute-start(f32[4,2048]{1,0:T(4,128)S(1)} %broadcast_select_fusion.6), channel_id=1, source_target_pairs={{0,4},{4,8},{8,12},{12,16},{16,20},{20,24},{24,28},{1,5},{5,9},{9,... | collective-permute-start | bytes 98312 | tf_op jit(solution)/shard_map/ppermute | solution.py:15
  97.1 6.0 %collective-permute-start.9 = (f32[4,2048]{1,0:T(4,128)S(1)}, f32[4,2048]{1,0:T(4,128)S(1)}, u32[]{:S(2)}, u32[]{:S(2)}) collective-permute-start(f32[4,2048]{1,0:T(4,128)S(1)} %broadcast_select_fusion.5), channel_id=1, source_target_pairs={{4,0},{8,4},{12,8},{16,12},{20,16},{24,20},{28,24},{5,1},{9,5},{13... | collective-permute-start | bytes 98312 | tf_op jit(solution)/shard_map/ppermute | solution.py:15
where the time goes:
time: 200 us; the launch traced here: 199 us
  blocking collectives  48.2 us (24%)
  matrix products  43.1 us (22%)
  local copies, waits for them, and re-layouts  42.5 us (21%)
  starting transfers between devices  33 us (16%)
  other arithmetic  28.2 us (14%)
  waiting for transfers between devices  2.87 us (1%)
    psum x1, blocking collectives, on_device(): partial_grams.append(lax.psum(local_block, ('fx', 'fy')))  48.2 us
    dot_general x3, matrix products, contract(): jnp.einsum('fkab,fkbr->far', block_mats, shaped, precision=lax.Precision....  36 us
    ppermute x12, starting transfers between devices, from_behind(): return lax.ppermute(block, axis, route)  33 us
    reshape x3, local copies, waits for them, and re-layouts, contract(): shaped = picked.reshape(face_count, picked.shape[1], DOF, NRHS)  12.3 us
    another operation x3, other arithmetic, solve_small(): factor = jnp.linalg.cholesky(normal_matrix)  9.45 us
    gather x6, local copies, waits for them, and re-layouts, on_device(): jnp.take(extended, face_columns, axis=0)  8.18 us
    another operation x2, other arithmetic, solve_small(): coeffs = jax.scipy.linalg.cho_solve((factor, True), right_terms)  8.01 us
    select_n x4, other arithmetic, on_device(): jnp.take(extended, face_columns, axis=0)  7.51 us
  transfers between devices with their start and end apart: 12, of which 1 were waited for; matrix products, arithmetic and copies ran while one was open for 9% of the time, Pallas kernels for 0%

commit v1 on v0

--- a/solution.py
+++ b/solution.py
@@ -67,7 +67,7 @@
         local_block = jnp.dot(
             earlier_rows.T, as_rows(fields[-1]), precision=high, preferred_element_type=jnp.float32
         )
-        partial_grams.append(lax.psum(local_block, ("fx", "fy")))
+        partial_grams.append(jnp.sum(lax.all_gather(local_block, ("fx", "fy")), axis=0))
     total_cols = (POWERS + 1) * NRHS
     upper_part = jnp.concatenate(
         [

time: 200 us -> 307 us (1.53)
  blocking collectives: 48.2 us -> 169 us
  starting transfers between devices: 33 us -> 24 us
    all_gather x0 -> x4, blocking collectives: none -> 169 us  [on_device(): lax.all_gather(local_block, ('fx', 'fy'))]
    psum x1 -> x0, blocking collectives: 48.2 us -> none  [on_device(): partial_grams.append(lax.psum(local_block, ('fx', 'fy')))]
    ppermute x12, starting transfers between devices: 33 us -> 24 us  [from_behind(): return lax.ppermute(block, axis, route)]
  transfers between devices with their start and end apart: 12 -> 12, of which waited for: 1 -> 0; matrix products, arithmetic and copies ran while one was open for 9% -> 5% of each run, Pallas kernels for 0% -> 0%
where the time goes in v1:
time: 307 us; the launch traced here: 306 us
  blocking collectives  169 us (55%)
  local copies, waits for them, and re-layouts  42.8 us (14%)
  matrix products  41.1 us (13%)
  other arithmetic  28.4 us (9%)
  starting transfers between devices  24 us (8%)
    all_gather x4, blocking collectives, on_device(): lax.all_gather(local_block, ('fx', 'fy'))  169 us
    dot_general x3, matrix products, contract(): jnp.einsum('fkab,fkbr->far', block_mats, shaped, precision=lax.Precision....  36 us
    ppermute x12, starting transfers between devices, from_behind(): return lax.ppermute(block, axis, route)  24 us
    reshape x3, local copies, waits for them, and re-layouts, contract(): shaped = picked.reshape(face_count, picked.shape[1], DOF, NRHS)  12.3 us
    another operation x3, other arithmetic, solve_small(): factor = jnp.linalg.cholesky(normal_matrix)  9.45 us
    gather x6, local copies, waits for them, and re-layouts, on_device(): jnp.take(extended, face_columns, axis=0)  8.18 us
    another operation x2, other arithmetic, solve_small(): coeffs = jax.scipy.linalg.cho_solve((factor, True), right_terms)  8.01 us
    select_n x4, other arithmetic, on_device(): jnp.take(extended, face_columns, axis=0)  7.5 us
  transfers between devices with their start and end apart: 12, of which 0 were waited for; matrix products, arithmetic and copies ran while one was open for 5% of the time, Pallas kernels for 0%

profile of v1, /device:TPU:0, one launch (start us, length us, event | category | flops | bytes accessed | tf_op | source)
XLA Modules:
  0.0 306.2 jit_solution(14876177268641244859)
XLA Ops:
  1.5 1.5 gather_fusion
  3.1 4.9 %collective-permute-start = (f32[4,2048]{1,0:T(4,128)S(1)}, f32[4,2048]{1,0:T(4,128)S(1)}, u32[]{:S(2)}, u32[]{:S(2)}) collective-permute-start(f32[4,2048]{1,0:T(4,128)S(1)} %broadcast_select_fusion.14), channel_id=1, source_target_pairs={{0,4},{4,8},{8,12},{12,16},{16,20},{20,24},{24,28},{1,5},{5,9},{9,... | collective-permute-start | bytes 98312 | tf_op jit(solution)/shard_map/ppermute | solution.py:15
  19.3 5.7 %reshape.92 = f32[16,11,64,64]{3,2,0,1:T(8,128)} reshape(f32[16,11,4096]{2,0,1:T(8,128)} %param.9) | data formatting | bytes 5767168 | tf_op jit(solution)/shard_map/reshape | solution.py:52
  26.0 47.2 %all-gather = f32[1024,32]{1,0:T(8,128)S(1)} all-gather(f32[32,32]{1,0:T(8,128)S(1)} %fusion.39), channel_id=2, replica_groups=mesh['fx'=8,'fy'=4] {'fx','fy'}, dimensions={0}, use_global_device_ids=true | all-gather | bytes 135168 | tf_op jit(solution)/shard_map/all_gather | solution.py:70
  74.6 1.5 reshape.258
  76.1 1.8 broadcast_select_fusion.2
  77.9 3.6 %reshape.286 = f32[16,11,64,32]{3,2,1,0:T(8,128)} reshape(f32[16,11,2048]{2,1,0:T(8,128)S(1)} %broadcast_select_fusion.2) | data formatting | bytes 2883584 | tf_op jit(solution)/shard_map/reshape | solution.py:28
  81.5 12.0 %fusion.6 = f32[16,64,32]{1,2,0:T(8,128)S(1)} fusion(f32[16,11,64,64]{3,2,0,1:T(8,128)} %reshape.92, f32[16,11,64,32]{3,2,1,0:T(8,128)} %reshape.286), kind=kOutput, calls=%fused_computation.21 | convolution fusion | flops 276824064 | bytes 4456448 | tf_op jit(solution)/shard_map/fkab,fkbr->far/dot_general | solution.py:29
  97.9 2.2 collective-permute-start.6
  101.5 4.3 %collective-permute-start.4 = (f32[4,2048]{1,0:T(4,128)S(1)}, f32[4,2048]{1,0:T(4,128)S(1)}, u32[]{:S(2)}, u32[]{:S(2)}) collective-permute-start(f32[4,2048]{1,0:T(4,128)S(1)} %broadcast_select_fusion.10), channel_id=1, source_target_pairs={{0,4},{4,8},{8,12},{12,16},{16,20},{20,24},{24,28},{1,5},{5,9},{9,... | collective-permute-start | bytes 98312 | tf_op jit(solution)/shard_map/ppermute | solution.py:15
  106.6 40.3 %all-gather.4 = f32[32,64,32]{1,2,0:T(8,128)S(1)} all-gather(f32[1,64,32]{1,2,0:T(8,128)S(1)} %convolution_bitcast_fusion.1), channel_id=3, replica_groups=mesh['fx'=8,'fy'=4] {'fx','fy'}, dimensions={0}, use_global_device_ids=true | all-gather | bytes 270336 | tf_op jit(solution)/shard_map/all_gather | solution.py:70
  148.3 1.5 reshape.270
  149.9 1.8 broadcast_select_fusion.1
  151.7 3.6 %reshape.287 = f32[16,11,64,32]{3,2,1,0:T(8,128)} reshape(f32[16,11,2048]{2,1,0:T(8,128)S(1)} %broadcast_select_fusion.1) | data formatting | bytes 2883584 | tf_op jit(solution)/shard_map/reshape | solution.py:28
  155.2 12.0 %fusion.9 = f32[16,64,32]{1,2,0:T(8,128)S(1)} fusion(f32[16,11,64,64]{3,2,0,1:T(8,128)} %reshape.92, f32[16,11,64,32]{3,2,1,0:T(8,128)} %reshape.287), kind=kOutput, calls=%fused_computation.22 | convolution fusion | flops 276824064 | bytes 4456448 | tf_op jit(solution)/shard_map/fkab,fkbr->far/dot_general | solution.py:29
  170.3 2.2 collective-permute-start.10
  177.6 42.9 %all-gather.5 = f32[32,96,32]{1,2,0:T(8,128)S(1)} all-gather(f32[1,96,32]{1,2,0:T(8,128)S(1)} %convolution_bitcast_fusion), channel_id=4, replica_groups=mesh['fx'=8,'fy'=4] {'fx','fy'}, dimensions={0}, use_global_device_ids=true | all-gather | bytes 405504 | tf_op jit(solution)/shard_map/all_gather | solution.py:70
  221.9 1.6 reshape.282
  223.6 3.2 %broadcast_select_fusion = f32[16,11,2048]{2,1,0:T(8,128)} fusion(f32[16,11,2048]{2,1,0:T(8,128)} %reshape.282, pred[16,11]{1,0:T(8,128)(4,1)S(1)} %compare_and_fusion), kind=kLoop, calls=%fused_computation.27 | loop fusion | flops 360448 | bytes 2883760 | tf_op jit(solution)/shard_map/jit(_take)/select_n | solution.py:65
  226.8 5.2 %reshape.288 = f32[16,11,64,32]{3,2,1,0:T(8,128)} reshape(f32[16,11,2048]{2,1,0:T(8,128)} %broadcast_select_fusion) | data formatting | bytes 2883584 | tf_op jit(solution)/shard_map/reshape | solution.py:28
  232.0 12.0 %fusion.12 = f32[16,64,32]{1,2,0:T(8,128)S(1)} fusion(f32[16,11,64,64]{3,2,0,1:T(8,128)} %reshape.92, f32[16,11,64,32]{3,2,1,0:T(8,128)} %reshape.288), kind=kOutput, calls=%fused_computation.23 | convolution fusion | flops 276824064 | bytes 4456448 | tf_op jit(solution)/shard_map/fkab,fkbr->far/dot_general | solution.py:29
  245.4 38.3 %all-gather.3 = f32[4096,32]{0,1:T(8,128)S(1)} all-gather(f32[128,32]{0,1:T(8,128)S(1)} %fusion.40), channel_id=5, replica_groups=mesh['fx'=8,'fy'=4] {'fx','fy'}, dimensions={0}, use_global_device_ids=true | all-gather | bytes 540672 | tf_op jit(solution)/shard_map/all_gather | solution.py:70
  285.1 8.8 %cholesky.16 = f32[96,96]{1,0:T(8,128)S(1)} custom-call(f32[96,96]{1,0:T(8,128)S(1)} %fusion.29), custom_call_target="Cholesky" | custom-call | tf_op jit(solution)/shard_map/jit(cholesky)/cholesky | solution.py:44
  295.2 7.4 %custom-call.10 = f32[1,96,96]{1,2,0:T(8,128)S(1)} custom-call(f32[1,96,96]{2,1,0:T(8,128)S(1)} %fusion.24), custom_call_target="InvertDiagBlocksLowerTriangular" | custom-call | tf_op jit(solution)/shard_map/jit(_cho_solve)/triangular_solve | solution.py:45
  (107 shorter events, 39.6 us)
Async XLA Ops:
  3.1 70.2 %collective-permute-start = (f32[4,2048]{1,0:T(4,128)S(1)}, f32[4,2048]{1,0:T(4,128)S(1)}, u32[]{:S(2)}, u32[]{:S(2)}) collective-permute-start(f32[4,2048]{1,0:T(4,128)S(1)} %broadcast_select_fusion.14), channel_id=1, source_target_pairs={{0,4},{4,8},{8,12},{12,16},{16,20},{20,24},{24,28},{1,5},{5,9},{9,... | collective-permute-start | bytes 98312 | tf_op jit(solution)/shard_map/ppermute | solution.py:15
  9.5 63.8 %collective-permute-start.1 = (f32[4,2048]{1,0:T(4,128)S(1)}, f32[4,2048]{1,0:T(4,128)S(1)}, u32[]{:S(2)}, u32[]{:S(2)}) collective-permute-start(f32[4,2048]{1,0:T(4,128)S(1)} %broadcast_select_fusion.13), channel_id=1, source_target_pairs={{4,0},{8,4},{12,8},{16,12},{20,16},{24,20},{28,24},{5,1},{9,5},{13... | collective-permute-start | bytes 98312 | tf_op jit(solution)/shard_map/ppermute | solution.py:15
  12.4 60.9 %collective-permute-start.2 = (f32[4,2048]{1,0:T(4,128)S(1)}, f32[4,2048]{1,0:T(4,128)S(1)}, u32[]{:S(2)}, u32[]{:S(2)}) collective-permute-start(f32[4,2048]{1,0:T(4,128)S(1)} %broadcast_select_fusion.12), channel_id=1, source_target_pairs={{0,1},{1,2},{2,3},{4,5},{5,6},{6,7},{8,9},{9,10},{10,11},{12,13},{... | collective-permute-start | bytes 98312 | tf_op jit(solution)/shard_map/ppermute | solution.py:15
  15.4 57.9 %collective-permute-start.3 = (f32[4,2048]{1,0:T(4,128)S(1)}, f32[4,2048]{1,0:T(4,128)S(1)}, u32[]{:S(2)}, u32[]{:S(2)}) collective-permute-start(f32[4,2048]{1,0:T(4,128)S(1)} %broadcast_select_fusion.11), channel_id=1, source_target_pairs={{1,0},{2,1},{3,2},{5,4},{6,5},{7,6},{9,8},{10,9},{11,10},{13,12},{... | collective-permute-start | bytes 98312 | tf_op jit(solution)/shard_map/ppermute | solution.py:15
  25.0 48.3 %copy-start = (f32[16,2048]{1,0:T(8,128)S(1)}, f32[16,2048]{1,0:T(8,128)}, u32[]{:S(2)}) copy-start(f32[16,2048]{1,0:T(8,128)} %param.8) | copy-start | bytes 393220
  96.5 50.6 %collective-permute-start.5 = (f32[4,2048]{1,0:T(4,128)S(1)}, f32[4,2048]{1,0:T(4,128)S(1)}, u32[]{:S(2)}, u32[]{:S(2)}) collective-permute-start(f32[4,2048]{1,0:T(4,128)S(1)} %broadcast_select_fusion.9), channel_id=1, source_target_pairs={{4,0},{8,4},{12,8},{16,12},{20,16},{24,20},{28,24},{5,1},{9,5},{13... | collective-permute-start | bytes 98312 | tf_op jit(solution)/shard_map/ppermute | solution.py:15
  97.9 49.2 %collective-permute-start.6 = (f32[4,2048]{1,0:T(4,128)S(1)}, f32[4,2048]{1,0:T(4,128)S(1)}, u32[]{:S(2)}, u32[]{:S(2)}) collective-permute-start(f32[4,2048]{1,0:T(4,128)S(1)} %broadcast_select_fusion.8), channel_id=1, source_target_pairs={{0,1},{1,2},{2,3},{4,5},{5,6},{6,7},{8,9},{9,10},{10,11},{12,13},{... | collective-permute-start | bytes 98312 | tf_op jit(solution)/shard_map/ppermute | solution.py:15
  100.2 46.9 %collective-permute-start.7 = (f32[4,2048]{1,0:T(4,128)S(1)}, f32[4,2048]{1,0:T(4,128)S(1)}, u32[]{:S(2)}, u32[]{:S(2)}) collective-permute-start(f32[4,2048]{1,0:T(4,128)S(1)} %broadcast_select_fusion.7), channel_id=1, source_target_pairs={{1,0},{2,1},{3,2},{5,4},{6,5},{7,6},{9,8},{10,9},{11,10},{13,12},{... | collective-permute-start | bytes 98312 | tf_op jit(solution)/shard_map/ppermute | solution.py:15
  101.5 45.5 %collective-permute-start.4 = (f32[4,2048]{1,0:T(4,128)S(1)}, f32[4,2048]{1,0:T(4,128)S(1)}, u32[]{:S(2)}, u32[]{:S(2)}) collective-permute-start(f32[4,2048]{1,0:T(4,128)S(1)} %broadcast_select_fusion.10), channel_id=1, source_target_pairs={{0,4},{4,8},{8,12},{12,16},{16,20},{20,24},{24,28},{1,5},{5,9},{9,... | collective-permute-start | bytes 98312 | tf_op jit(solution)/shard_map/ppermute | solution.py:15
  170.3 50.4 %collective-permute-start.10 = (f32[4,2048]{1,0:T(4,128)S(1)}, f32[4,2048]{1,0:T(4,128)S(1)}, u32[]{:S(2)}, u32[]{:S(2)}) collective-permute-start(f32[4,2048]{1,0:T(4,128)S(1)} %broadcast_select_fusion.4), channel_id=1, source_target_pairs={{0,1},{1,2},{2,3},{4,5},{5,6},{6,7},{8,9},{9,10},{10,11},{12,13},{... | collective-permute-start | bytes 98312 | tf_op jit(solution)/shard_map/ppermute | solution.py:15
  172.6 48.1 %collective-permute-start.11 = (f32[4,2048]{1,0:T(4,128)S(1)}, f32[4,2048]{1,0:T(4,128)S(1)}, u32[]{:S(2)}, u32[]{:S(2)}) collective-permute-start(f32[4,2048]{1,0:T(4,128)S(1)} %broadcast_select_fusion.3), channel_id=1, source_target_pairs={{1,0},{2,1},{3,2},{5,4},{6,5},{7,6},{9,8},{10,9},{11,10},{13,12},{... | collective-permute-start | bytes 98312 | tf_op jit(solution)/shard_map/ppermute | solution.py:15
  173.9 46.7 %collective-permute-start.8 = (f32[4,2048]{1,0:T(4,128)S(1)}, f32[4,2048]{1,0:T(4,128)S(1)}, u32[]{:S(2)}, u32[]{:S(2)}) collective-permute-start(f32[4,2048]{1,0:T(4,128)S(1)} %broadcast_select_fusion.6), channel_id=1, source_target_pairs={{0,4},{4,8},{8,12},{12,16},{16,20},{20,24},{24,28},{1,5},{5,9},{9,... | collective-permute-start | bytes 98312 | tf_op jit(solution)/shard_map/ppermute | solution.py:15
  175.3 45.4 %collective-permute-start.9 = (f32[4,2048]{1,0:T(4,128)S(1)}, f32[4,2048]{1,0:T(4,128)S(1)}, u32[]{:S(2)}, u32[]{:S(2)}) collective-permute-start(f32[4,2048]{1,0:T(4,128)S(1)} %broadcast_select_fusion.5), channel_id=1, source_target_pairs={{4,0},{8,4},{12,8},{16,12},{20,16},{24,20},{28,24},{5,1},{9,5},{13... | collective-permute-start | bytes 98312 | tf_op jit(solution)/shard_map/ppermute | solution.py:15
